TPU v7x, 256 devices: a whole 4x4x8 slice. The times are simulated.
256 devices in a mesh: pool: 16 (over z, core), tensor: 16 (over y, x).
Axes of the slice: x: 4, y: 4, z: 8, core: 2. Of those that a mesh axis runs over, the one named last changes fastest.
Arguments:
- hidden: bfloat16 [8192, 14336], P('pool', 'tensor'), may hold values from -6 to 6
- down_weight: bfloat16 [14336, 8192], P('tensor', 'pool'), may hold values from -0.046875 to 0.046875
- adapter_shrink: bfloat16 [32, 14336, 64], P('pool', 'tensor'), may hold values from -0.046875 to 0.046875
- adapter_expand: bfloat16 [32, 8192, 64], P('pool', 'tensor'), may hold values from -0.75 to 0.75
- block_adapter: int32 [64], P('pool'), may hold values from 0 to 31, as said below
- block_rows: int32 [64], P('pool'), may hold values from 1 to 128, 6144 in all
Outputs:
- projected: bfloat16 [8192, 8192], P(('pool', 'tensor'))
Inputs may be any that keep to these rules, and one draw needn't show every extreme that they name: `block_adapter`: within each aligned run of 4 blocks (the rows of one pool index) no two blocks name adapters with the same a // 2. `block_rows`: some block is full.
All inputs are finite; a program needn't handle non-finite values.
Results may differ from a plain program's by a relative error of at most 0.02.
Values may be sent and summed in bfloat16 or wider, within the bound.
A program may use at most 128 MiB of HBM per device.

v0:
```python
import jax
import jax.numpy as jnp
from jax import lax
from jax.sharding import PartitionSpec as P

BLOCK = 128
adapter_scale_factor = 0.5


def shards(hidden, down_weight, adapter_shrink, adapter_expand, block_adapter, block_rows):
    input_rows, feat = hidden.shape
    block_count = block_adapter.shape[0]
    column_span = adapter_expand.shape[1]
    tensor_pos = lax.axis_index("tensor")
    tensor_count = lax.axis_size("tensor")
    own_rows = input_rows // tensor_count
    blocks = hidden.reshape(block_count, BLOCK, feat)
    partial_value = jnp.dot(
        hidden,
        lax.all_gather(down_weight, "pool", axis=1, tiled=True),
        preferred_element_type=jnp.float32,
    )
    total = lax.psum_scatter(
        partial_value.astype(jnp.bfloat16), "tensor", scatter_dimension=0, tiled=True
    ).astype(jnp.float32)
    shrink_piece = lax.all_gather(adapter_shrink, "pool", axis=0, tiled=True)
    expand_piece = lax.all_gather(adapter_expand, "pool", axis=0, tiled=True)
    idents = jnp.arange(shrink_piece.shape[0], dtype=jnp.int32)
    pick = (block_adapter[:, None] == idents[None, :]).astype(jnp.bfloat16)
    first = jnp.einsum("bk,kfr->bfr", pick, shrink_piece, preferred_element_type=jnp.float32)
    second = jnp.einsum("bk,kcr->bcr", pick, expand_piece, preferred_element_type=jnp.float32)
    shrink = jnp.einsum(
        "bnf,bfr->bnr", blocks, first.astype(jnp.bfloat16), preferred_element_type=jnp.float32
    )
    summed_shrink = lax.psum(shrink.astype(jnp.bfloat16), "tensor")
    enlarged_rows = jnp.einsum(
        "bnr,bcr->bnc",
        summed_shrink,
        second.astype(jnp.bfloat16),
        preferred_element_type=jnp.float32,
    )
    adapter_delta_columns = (
        (adapter_scale_factor * enlarged_rows).astype(jnp.bfloat16).reshape(input_rows, column_span)
    )
    delta_mine = lax.all_to_all(
        adapter_delta_columns, "tensor", split_axis=0, concat_axis=1, tiled=True
    )
    total = total + delta_mine.astype(jnp.float32)
    row_ids = tensor_pos * own_rows + jnp.arange(own_rows, dtype=jnp.int32)
    owning = (row_ids // BLOCK)[:, None] == jnp.arange(block_count, dtype=jnp.int32)[None, :]
    lengths = jnp.sum(jnp.where(owning, block_rows[None, :], 0), axis=1)
    valid = (row_ids % BLOCK < lengths).astype(jnp.float32)
    return (total * valid[:, None]).astype(jnp.bfloat16)


def solution(mesh):
    in_specs = (
        P("pool", "tensor"),
        P("tensor", "pool"),
        P("pool", "tensor", None),
        P("pool", "tensor", None),
        P("pool"),
        P("pool"),
    )
    out_specs = P(("pool", "tensor"), None)
    return jax.shard_map(shards, mesh=mesh, in_specs=in_specs, out_specs=out_specs, check_vma=False)
```

profile of v0, /device:TPU:2, one launch (start us, length us, event | category | flops | bytes accessed | tf_op | source)
XLA Modules:
  0.0 374.3 jit_solution(14904361085306204502)
XLA Ops:
  6.5 0.0 copy-start
  6.5 0.0 all-gather.6.cloned.1.call-start
  6.5 0.7 all-gather.6.cloned.1.call-update
  7.3 0.0 all-gather.4.cloned.1.call-start
  7.3 0.7 all-gather.4.cloned.1.call-update
  8.0 0.0 all-gather.8.cloned.1.call-start
  8.1 0.7 all-gather.8.cloned.1.call-update
  8.7 0.0 all-reduce.2.cloned.1.call-start
  8.8 45.0 %all-gather.6.cloned.1.call-done = bf16[32,896,64]{1,2,0:T(8,128)(2,1)} async-done(((bf16[2,896,64]{1,2,0:T(8,128)(2,1)}), bf16[32,896,64]{1,2,0:T(8,128)(2,1)}) %all-gather.6.cloned.1.call-update) | async-done | bytes 3670032 | tf_op jit(solution)/shard_map/all_gather | solution.py:26
  53.8 5.0 %fusion.5 = bf16[4,896,64]{1,0,2:T(4,128)(2,1)S(1)} fusion(bf16[32,896,64]{1,2,0:T(8,128)(2,1)} %all-gather.6.cloned.1.call-done, s32[4]{0:T(128)} %param.10), kind=kOutput, calls=%fused_computation.7 | convolution fusion | flops 14909568 | bytes 4128784 | tf_op jit(solution)/shard_map/bk,kfr->bfr/dot_general | solution.py:30
  58.8 0.0 copy-done
  58.8 1.1 fusion.11
  59.9 0.0 all-reduce.2.cloned.1.call-update
  59.9 0.0 reduce-scatter.2.cloned.1.call-start
  59.9 79.8 %all-gather.4.cloned.1.call-done = bf16[896,8192]{1,0:T(8,128)(2,1)} async-done(((bf16[896,512]{1,0:T(8,128)(2,1)}), bf16[896,8192]{1,0:T(8,128)(2,1)}) %all-gather.4.cloned.1.call-update) | async-done | bytes 14680080 | tf_op jit(solution)/shard_map/all_gather | solution.py:20
  139.8 16.5 %convolution_convert_fusion = bf16[512,8192]{1,0:T(8,128)(2,1)} fusion(bf16[512,896]{1,0:T(8,128)(2,1)S(1)} %copy-done, bf16[896,8192]{1,0:T(8,128)(2,1)} %all-gather.4.cloned.1.call-done), kind=kOutput, calls=%fused_computation | convolution fusion | flops 7520387072 | bytes 23986176 | tf_op jit(solution)/shard_map/dot_general | solution.py:18
  156.3 0.0 copy-start.1
  156.3 0.0 reduce-scatter.2.cloned.1.call-update
  156.3 0.0 copy-start.2
  156.3 23.6 %all-gather.8.cloned.1.call-done = bf16[32,512,64]{1,2,0:T(8,128)(2,1)} async-done(((bf16[2,512,64]{1,2,0:T(8,128)(2,1)}), bf16[32,512,64]{1,2,0:T(8,128)(2,1)}) %all-gather.8.cloned.1.call-update) | async-done | bytes 2097168 | tf_op jit(solution)/shard_map/all_gather | solution.py:27
  179.9 0.0 copy-done.1
  179.9 2.9 fusion.8
  182.8 89.2 %all-reduce.2.cloned.1.call-done = bf16[4,128,64]{1,2,0:T(8,128)(2,1)} async-done(((bf16[4,128,64]{1,2,0:T(8,128)(2,1)}), bf16[4,128,64]{1,2,0:T(8,128)(2,1)}) %all-reduce.2.cloned.1.call-update) | async-done | bytes 65552 | tf_op jit(solution)/shard_map/psum | solution.py:35
  272.0 2.0 fusion.4
  274.0 5.7 %all-to-all-start = ((bf16[16,32,512]{2,1,0:T(8,128)(2,1)}), bf16[16,32,512]{2,1,0:T(8,128)(2,1)S(1)}, u32[]{:S(2)}, u32[]{:S(2)}) async-start(bf16[16,32,512]{2,1,0:T(8,128)(2,1)} %bitcast.3), calls=%async_computation.1 | async-start | bytes 1048576 | tf_op jit(solution)/shard_map/all_to_all | solution.py:45
  279.7 0.0 copy-done.2
  279.8 0.1 select_reduce_fusion
  279.9 8.6 %all-to-all-done = bf16[16,32,512]{2,1,0:T(8,128)(2,1)S(1)} async-done(((bf16[16,32,512]{2,1,0:T(8,128)(2,1)}), bf16[16,32,512]{2,1,0:T(8,128)(2,1)S(1)}, u32[]{:S(2)}, u32[]{:S(2)}) %all-to-all-start) | async-done | bytes 524320 | tf_op jit(solution)/shard_map/all_to_all | solution.py:45
  288.5 0.1 convert_bitcast_fusion
  288.6 0.1 copy.14
  288.7 77.0 %reduce-scatter.2.cloned.1.call-done = bf16[32,8192]{1,0:T(8,128)(2,1)} async-done(((bf16[512,8192]{1,0:T(8,128)(2,1)}), bf16[32,8192]{1,0:T(8,128)(2,1)}) %reduce-scatter.2.cloned.1.call-update) | async-done | bytes 524304 | tf_op jit(solution)/shard_map/reduce_scatter | solution.py:23
  365.7 2.0 multiply_convert_fusion
  (2 shorter events, 0.0 us)
Async XLA Ops:
  6.5 52.2 %copy-start = (bf16[512,896]{1,0:T(8,128)(2,1)S(1)}, bf16[512,896]{1,0:T(8,128)(2,1)}, u32[]{:S(2)}) copy-start(bf16[512,896]{1,0:T(8,128)(2,1)} %param.6) | copy-start | bytes 2752516
  6.5 47.2 %all-gather.6.cloned.1.call-start = ((), (), s32[]{:S(2)}) async-start(), calls=%async_computation.4 | async-start | bytes 3899392 | tf_op jit(solution)/shard_map/all_gather | solution.py:26
  7.3 132.5 %all-gather.4.cloned.1.call-start = ((), (), s32[]{:S(2)}) async-start(), calls=%async_computation.2 | async-start | bytes 15597568 | tf_op jit(solution)/shard_map/all_gather | solution.py:20
  8.0 171.9 %all-gather.8.cloned.1.call-start = ((), (), s32[]{:S(2)}) async-start(), calls=%async_computation.6 | async-start | bytes 2228224 | tf_op jit(solution)/shard_map/all_gather | solution.py:27
  8.7 263.3 %all-reduce.2.cloned.1.call-start = ((), (), s32[]{:S(2)}) async-start(), calls=%async_computation.5 | async-start | bytes 131072 | tf_op jit(solution)/shard_map/psum | solution.py:35
  59.9 305.8 %reduce-scatter.2.cloned.1.call-start = ((), (), s32[]{:S(2)}) async-start(), calls=%async_computation.3 | async-start | bytes 8912896 | tf_op jit(solution)/shard_map/reduce_scatter | solution.py:23
  156.3 23.6 %copy-start.1 = (s32[4]{0:T(128)S(1)}, s32[4]{0:T(128)}, u32[]{:S(2)}) copy-start(s32[4]{0:T(128)} %param.10) | copy-start | bytes 52
  156.3 123.4 %copy-start.2 = (s32[4]{0:T(128)S(1)}, s32[4]{0:T(128)}, u32[]{:S(2)}) copy-start(s32[4]{0:T(128)} %param.11) | copy-start | bytes 52
  274.0 14.5 %all-to-all-start = ((bf16[16,32,512]{2,1,0:T(8,128)(2,1)}), bf16[16,32,512]{2,1,0:T(8,128)(2,1)S(1)}, u32[]{:S(2)}, u32[]{:S(2)}) async-start(bf16[16,32,512]{2,1,0:T(8,128)(2,1)} %bitcast.3), calls=%async_computation.1 | async-start | bytes 1048576 | tf_op jit(solution)/shard_map/all_to_all | solution.py:45
Sparse Core Ops, SparseCore 0:
  9.2 44.5 all-gather.5
  55.6 84.1 all-gather.3
  141.6 38.2 all-gather.7
  183.0 89.0 all-reduce.1
  276.0 89.6 reduce-scatter.1
where the time goes:
time: 375 us; the launch traced here: 374 us
  waiting for transfers between devices  325 us (87%)
  matrix products  27.4 us (7%)
  between operations  13.2 us (4%)
  starting transfers between devices  5.89 us (2%)
    psum x1, waiting for transfers between devices, shards(): summed_shrink = lax.psum(shrink.astype(jnp.bfloat16), 'tensor')  89.2 us
    all_gather x1, waiting for transfers between devices, shards(): lax.all_gather(down_weight, 'pool', axis=1, tiled=True)  79.8 us
    reduce_scatter x1, waiting for transfers between devices, shards(): lax.psum_scatter(partial_value.astype(jnp.bfloat16), 'tensor', scatter_di...  77 us
    all_gather x1, waiting for transfers between devices, shards(): shrink_piece = lax.all_gather(adapter_shrink, 'pool', axis=0, tiled=True)  45 us
    all_gather x1, waiting for transfers between devices, shards(): expand_piece = lax.all_gather(adapter_expand, 'pool', axis=0, tiled=True)  23.6 us
    dot_general x1, matrix products, shards(): jnp.dot(hidden, lax.all_gather(down_weight, 'pool', axis=1, tiled=True),...  16.5 us
    all_to_all x1, waiting for transfers between devices, shards(): lax.all_to_all(adapter_delta_columns, 'tensor', split_axis=0, concat_axis...  8.61 us
  transfers between devices with their start and end apart: 6, of which 6 were waited for; matrix products, arithmetic and copies ran while one was open for 7% of the time, Pallas kernels for 0%

commit v1 on v0

--- a/solution.py
+++ b/solution.py
@@ -23,7 +23,10 @@
     total = lax.psum_scatter(
         partial_value.astype(jnp.bfloat16), "tensor", scatter_dimension=0, tiled=True
     ).astype(jnp.float32)
-    shrink_piece = lax.all_gather(adapter_shrink, "pool", axis=0, tiled=True)
+    count = lax.axis_size("pool")
+    tiles = jnp.stack([adapter_shrink for _ in range(count)])
+    tiles = lax.all_to_all(tiles, "pool", split_axis=0, concat_axis=0)
+    shrink_piece = jnp.concatenate(tiles, axis=0)
     expand_piece = lax.all_gather(adapter_expand, "pool", axis=0, tiled=True)
     idents = jnp.arange(shrink_piece.shape[0], dtype=jnp.int32)
     pick = (block_adapter[:, None] == idents[None, :]).astype(jnp.bfloat16)

time: 375 us -> 340 us (0.907)
  waiting for transfers between devices: 325 us -> 277 us
  starting transfers between devices: 5.89 us -> 14.6 us
    all_to_all x0 -> x1, waiting for transfers between devices: none -> 118 us  [shards(): tiles = lax.all_to_all(tiles, 'pool', split_axis=0, concat_axis=0)]
    psum x1, waiting for transfers between devices: 89.2 us -> 18.8 us  [shards(): summed_shrink = lax.psum(shrink.astype(jnp.bfloat16), 'tensor')]
    all_gather x1, waiting for transfers between devices: 79.8 us -> 28.1 us  [shards(): lax.all_gather(down_weight, 'pool', axis=1, tiled=True)]
    all_gather x1 -> x0, waiting for transfers between devices: 45 us -> none  [shards(): shrink_piece = lax.all_gather(adapter_shrink, 'pool', axis=0, tiled=True)]
    all_to_all x0 -> x1, starting transfers between devices: none -> 8.75 us  [shards(): tiles = lax.all_to_all(tiles, 'pool', split_axis=0, concat_axis=0)]
  transfers between devices with their start and end apart: 6 -> 6, of which waited for: 6 -> 6; matrix products, arithmetic and copies ran while one was open for 7% -> 9% of each run, Pallas kernels for 0% -> 0%
where the time goes in v1:
time: 340 us
  waiting for transfers between devices  277 us (81%)
  matrix products  27.5 us (8%)
  between operations  14.9 us (4%)
  starting transfers between devices  14.6 us (4%)
    all_to_all x1, waiting for transfers between devices, shards(): tiles = lax.all_to_all(tiles, 'pool', split_axis=0, concat_axis=0)  118 us
    reduce_scatter x1, waiting for transfers between devices, shards(): lax.psum_scatter(partial_value.astype(jnp.bfloat16), 'tensor', scatter_di...  77.3 us
    all_gather x1, waiting for transfers between devices, shards(): lax.all_gather(down_weight, 'pool', axis=1, tiled=True)  28.1 us
    all_gather x1, waiting for transfers between devices, shards(): expand_piece = lax.all_gather(adapter_expand, 'pool', axis=0, tiled=True)  24.4 us
    psum x1, waiting for transfers between devices, shards(): summed_shrink = lax.psum(shrink.astype(jnp.bfloat16), 'tensor')  18.8 us
    dot_general x1, matrix products, shards(): jnp.dot(hidden, lax.all_gather(down_weight, 'pool', axis=1, tiled=True),...  16.5 us
    all_to_all x1, starting transfers between devices, shards(): tiles = lax.all_to_all(tiles, 'pool', split_axis=0, concat_axis=0)  8.75 us
    all_to_all x1, waiting for transfers between devices, shards(): lax.all_to_all(adapter_delta_columns, 'tensor', split_axis=0, concat_axis...  8.61 us
  transfers between devices with their start and end apart: 6, of which 6 were waited for; matrix products, arithmetic and copies ran while one was open for 9% of the time, Pallas kernels for 0%

profile of v1, /device:TPU:2, one launch (start us, length us, event | category | flops | bytes accessed | tf_op | source)
XLA Modules:
  0.0 339.6 jit_solution(8874728989844227881)
XLA Ops:
  7.4 0.0 copy-start
  7.4 0.0 all-gather.3.cloned.1.call-start
  7.4 0.7 all-gather.3.cloned.1.call-update
  8.1 3.3 stack.2
  11.4 0.0 copy-start.1
  11.4 8.7 %all-to-all-start = ((bf16[16,2,896,64]{2,3,1,0:T(8,128)(2,1)}), bf16[16,2,896,64]{2,3,1,0:T(8,128)(2,1)}, u32[]{:S(2)}, u32[]{:S(2)}) async-start(bf16[16,2,896,64]{2,3,1,0:T(8,128)(2,1)} %stack.2), calls=%async_computation.1 | async-start | bytes 7340032 | tf_op jit(solution)/shard_map/all_to_all | solution.py:28
  20.1 0.0 all-gather.5.cloned.1.call-start
  20.2 0.7 all-gather.5.cloned.1.call-update
  20.9 0.0 all-reduce.2.cloned.1.call-start
  20.9 118.4 %all-to-all-done = bf16[16,2,896,64]{2,3,1,0:T(8,128)(2,1)} async-done(((bf16[16,2,896,64]{2,3,1,0:T(8,128)(2,1)}), bf16[16,2,896,64]{2,3,1,0:T(8,128)(2,1)}, u32[]{:S(2)}, u32[]{:S(2)}) %all-to-all-start) | async-done | bytes 3670048 | tf_op jit(solution)/shard_map/all_to_all | solution.py:28
  139.4 0.0 copy-done.1
  139.4 5.1 %fusion.5 = bf16[4,896,64]{1,0,2:T(4,128)(2,1)S(1)} fusion(bf16[32,896,64]{1,2,0:T(8,128)(2,1)} %bitcast.1, s32[4]{0:T(128)S(1)} %copy-done.1), kind=kOutput, calls=%fused_computation.7 | convolution fusion | flops 14909568 | bytes 4128784 | tf_op jit(solution)/shard_map/bk,kfr->bfr/dot_general | solution.py:33
  144.5 0.0 copy-done
  144.5 1.1 fusion.11
  145.6 0.0 all-reduce.2.cloned.1.call-update
  145.6 0.0 reduce-scatter.2.cloned.1.call-start
  145.6 28.1 %all-gather.3.cloned.1.call-done = bf16[896,8192]{1,0:T(8,128)(2,1)} async-done(((bf16[896,512]{1,0:T(8,128)(2,1)}), bf16[896,8192]{1,0:T(8,128)(2,1)}) %all-gather.3.cloned.1.call-update) | async-done | bytes 14680080 | tf_op jit(solution)/shard_map/all_gather | solution.py:20
  173.7 16.5 %convolution_convert_fusion = bf16[512,8192]{1,0:T(8,128)(2,1)} fusion(bf16[512,896]{1,0:T(8,128)(2,1)S(1)} %copy-done, bf16[896,8192]{1,0:T(8,128)(2,1)} %all-gather.3.cloned.1.call-done), kind=kOutput, calls=%fused_computation | convolution fusion | flops 7520387072 | bytes 23986176 | tf_op jit(solution)/shard_map/dot_general | solution.py:18
  190.2 0.0 reduce-scatter.2.cloned.1.call-update
  190.3 0.0 copy-start.2
  190.3 24.4 %all-gather.5.cloned.1.call-done = bf16[32,512,64]{1,2,0:T(8,128)(2,1)} async-done(((bf16[2,512,64]{1,2,0:T(8,128)(2,1)}), bf16[32,512,64]{1,2,0:T(8,128)(2,1)}) %all-gather.5.cloned.1.call-update) | async-done | bytes 2097168 | tf_op jit(solution)/shard_map/all_gather | solution.py:30
  214.6 2.9 fusion.8
  217.5 18.8 %all-reduce.2.cloned.1.call-done = bf16[4,128,64]{1,2,0:T(8,128)(2,1)} async-done(((bf16[4,128,64]{1,2,0:T(8,128)(2,1)}), bf16[4,128,64]{1,2,0:T(8,128)(2,1)}) %all-reduce.2.cloned.1.call-update) | async-done | bytes 65552 | tf_op jit(solution)/shard_map/psum | solution.py:38
  236.3 2.0 fusion.4
  238.2 5.7 %all-to-all-start.1 = ((bf16[16,32,512]{2,1,0:T(8,128)(2,1)}), bf16[16,32,512]{2,1,0:T(8,128)(2,1)S(1)}, u32[]{:S(2)}, u32[]{:S(2)}) async-start(bf16[16,32,512]{2,1,0:T(8,128)(2,1)} %bitcast.4), calls=%async_computation.2 | async-start | bytes 1048576 | tf_op jit(solution)/shard_map/all_to_all | solution.py:48
  244.0 0.0 copy-done.2
  244.0 0.1 select_reduce_fusion
  244.1 8.6 %all-to-all-done.1 = bf16[16,32,512]{2,1,0:T(8,128)(2,1)S(1)} async-done(((bf16[16,32,512]{2,1,0:T(8,128)(2,1)}), bf16[16,32,512]{2,1,0:T(8,128)(2,1)S(1)}, u32[]{:S(2)}, u32[]{:S(2)}) %all-to-all-start.1) | async-done | bytes 524320 | tf_op jit(solution)/shard_map/all_to_all | solution.py:48
  252.7 0.1 convert_bitcast_fusion
  252.8 0.1 copy.16
  252.9 77.3 %reduce-scatter.2.cloned.1.call-done = bf16[32,8192]{1,0:T(8,128)(2,1)} async-done(((bf16[512,8192]{1,0:T(8,128)(2,1)}), bf16[32,8192]{1,0:T(8,128)(2,1)}) %reduce-scatter.2.cloned.1.call-update) | async-done | bytes 524304 | tf_op jit(solution)/shard_map/reduce_scatter | solution.py:23
  330.2 2.0 multiply_convert_fusion
  (2 shorter events, 0.0 us)
Async XLA Ops:
  7.4 137.1 %copy-start = (bf16[512,896]{1,0:T(8,128)(2,1)S(1)}, bf16[512,896]{1,0:T(8,128)(2,1)}, u32[]{:S(2)}) copy-start(bf16[512,896]{1,0:T(8,128)(2,1)} %param.6) | copy-start | bytes 2752516
  7.4 166.4 %all-gather.3.cloned.1.call-start = ((), (), s32[]{:S(2)}) async-start(), calls=%async_computation.3 | async-start | bytes 15597568 | tf_op jit(solution)/shard_map/all_gather | solution.py:20
  11.4 128.0 %copy-start.1 = (s32[4]{0:T(128)S(1)}, s32[4]{0:T(128)}, u32[]{:S(2)}) copy-start(s32[4]{0:T(128)} %param.10) | copy-start | bytes 52
  11.4 128.0 %all-to-all-start = ((bf16[16,2,896,64]{2,3,1,0:T(8,128)(2,1)}), bf16[16,2,896,64]{2,3,1,0:T(8,128)(2,1)}, u32[]{:S(2)}, u32[]{:S(2)}) async-start(bf16[16,2,896,64]{2,3,1,0:T(8,128)(2,1)} %stack.2), calls=%async_computation.1 | async-start | bytes 7340032 | tf_op jit(solution)/shard_map/all_to_all | solution.py:28
  20.1 194.5 %all-gather.5.cloned.1.call-start = ((), (), s32[]{:S(2)}) async-start(), calls=%async_computation.6 | async-start | bytes 2228224 | tf_op jit(solution)/shard_map/all_gather | solution.py:30
  20.9 215.4 %all-reduce.2.cloned.1.call-start = ((), (), s32[]{:S(2)}) async-start(), calls=%async_computation.5 | async-start | bytes 131072 | tf_op jit(solution)/shard_map/psum | solution.py:38
  145.6 184.6 %reduce-scatter.2.cloned.1.call-start = ((), (), s32[]{:S(2)}) async-start(), calls=%async_computation.4 | async-start | bytes 8912896 | tf_op jit(solution)/shard_map/reduce_scatter | solution.py:23
  190.3 53.7 %copy-start.2 = (s32[4]{0:T(128)S(1)}, s32[4]{0:T(128)}, u32[]{:S(2)}) copy-start(s32[4]{0:T(128)} %param.11) | copy-start | bytes 52
  238.2 14.5 %all-to-all-start.1 = ((bf16[16,32,512]{2,1,0:T(8,128)(2,1)}), bf16[16,32,512]{2,1,0:T(8,128)(2,1)S(1)}, u32[]{:S(2)}, u32[]{:S(2)}) async-start(bf16[16,32,512]{2,1,0:T(8,128)(2,1)} %bitcast.4), calls=%async_computation.2 | async-start | bytes 1048576 | tf_op jit(solution)/shard_map/all_to_all | solution.py:48
Sparse Core Ops, SparseCore 0:
  10.2 163.5 all-gather.2
  175.7 38.8 all-gather.4
Sparse Core Ops, SparseCore 1:
  145.7 90.5 all-reduce.1
  240.3 89.8 reduce-scatter.1
